TPU v7x, 32 devices: a whole 2x2x4 slice. The times are simulated.
32 devices in a mesh: shard: 8 (over z, core), rep: 4 (over y, x).
Axes of the slice: x: 2, y: 2, z: 4, core: 2. Of those that a mesh axis runs over, the one named last changes fastest.
Arguments:
- tokens: bfloat16 [2, 8192, 1024], P(None, ('shard', 'rep')), may hold values from -6 to 6
- cotangent: bfloat16 [2, 8192, 1024], P(None, ('shard', 'rep')), may hold values from -6 to 6
- seq_lengths: int32 [2, 4, 8, 4], P(None, 'rep'), may hold values from 1 to 128, 256 in all within a row
- dealing: int32 [2, 4, 32], P(None, 'rep'), may hold values from 0 to 31, each once within a row
- attention_gain: bfloat16 [1024], P('shard'), may hold values from 0.25 to 1.75
- attention_shift: bfloat16 [1024], P('shard'), may hold values from -1 to 1
- input_weight: bfloat16 [1024, 3072], P('shard'), may hold values from -0.25 to 0.25
- query_bias: bfloat16 [1024], P('shard'), may hold values from -1 to 1
- value_bias: bfloat16 [1024], P('shard'), may hold values from -1 to 1
- output_weight: bfloat16 [1024, 1024], P('shard'), may hold values from -0.5 to 0.5
- output_bias: bfloat16 [1024], P('shard'), may hold values from -1 to 1
- feed_gain: bfloat16 [1024], P('shard'), may hold values from 0.25 to 1.75
- feed_shift: bfloat16 [1024], P('shard'), may hold values from -1 to 1
- up_weight: bfloat16 [1024, 4096], P('shard'), may hold values from -0.1875 to 0.1875
- up_bias: bfloat16 [4096], P('shard'), may hold values from -1 to 1
- down_weight: bfloat16 [4096, 1024], P('shard'), may hold values from -0.09375 to 0.09375
- down_bias: bfloat16 [1024], P('shard'), may hold values from -1 to 1
Outputs:
- block_out: bfloat16 [2, 8192, 1024], P(None, ('shard', 'rep'))
- input_grad: bfloat16 [2, 8192, 1024], P(None, ('shard', 'rep'))
- attention_gain_grad: float32 [1024], P('shard')
- attention_shift_grad: float32 [1024], P('shard')
- input_weight_grad: float32 [1024, 3072], P('shard')
- query_bias_grad: float32 [1024], P('shard')
- value_bias_grad: float32 [1024], P('shard')
- output_weight_grad: float32 [1024, 1024], P('shard')
- output_bias_grad: float32 [1024], P('shard')
- feed_gain_grad: float32 [1024], P('shard')
- feed_shift_grad: float32 [1024], P('shard')
- up_weight_grad: float32 [1024, 4096], P('shard')
- up_bias_grad: float32 [4096], P('shard')
- down_weight_grad: float32 [4096, 1024], P('shard')
- down_bias_grad: float32 [1024], P('shard')
Inputs may be any that keep to these rules, and one draw needn't show every extreme that they name: `seq_lengths`: for every micro-batch and replica, the 4 lengths given for each index of shard add up to 256. `dealing`: for every micro-batch and replica, each dealt number appears once; number n goes to index n // 4 of shard.
All inputs are finite; a program needn't handle non-finite values.
Results may differ from a plain program's by a relative error of at most 0.013.
The roundings to bfloat16 on the way count: a program that leaves them out, or rounds other values in their place, can miss the bound.
Values may be sent and summed in bfloat16 or wider, within the bound.
A program may use at most 256 MiB of HBM per device.

v0:
```python
from functools import partial
import jax
import jax.numpy as jnp
from jax import lax
from jax.sharding import PartitionSpec as P

HD = 64
EPSILON = 1e-05
MASKED = -1e30


def deal_maps(seq_lengths, dealing, rows_dev):
    groups, per_device = seq_lengths.shape
    total_seqs = groups * per_device
    numbers = jnp.arange(total_seqs, dtype=jnp.int32)
    flat_lengths = seq_lengths.reshape(total_seqs)
    matched = (dealing[:, None] == numbers[None, :]).astype(jnp.int32)
    packed_length = jnp.sum(matched * flat_lengths[None, :], axis=1, dtype=jnp.int32)
    packed_start = jnp.cumsum(packed_length, dtype=jnp.int32) - packed_length
    start_of = jnp.sum(matched * packed_start[:, None], axis=0, dtype=jnp.int32).reshape(
        groups, per_device
    )
    bin_start = jnp.cumsum(seq_lengths, axis=1, dtype=jnp.int32) - seq_lengths
    places = jnp.arange(rows_dev, dtype=jnp.int32)
    inside = (places[None, :, None] >= bin_start[:, None, :]).astype(jnp.int32)
    segment = jnp.sum(inside, axis=2, dtype=jnp.int32) - 1
    picked = (segment[:, :, None] == jnp.arange(per_device, dtype=jnp.int32)[None, None, :]).astype(
        jnp.int32
    )
    position = places[None, :] - jnp.sum(picked * bin_start[:, None, :], axis=2, dtype=jnp.int32)
    source = jnp.sum(picked * start_of[:, None, :], axis=2, dtype=jnp.int32) + position
    total_rows = groups * rows_dev
    all_rows = jnp.arange(total_rows, dtype=jnp.int32)
    owner_seq = (
        jnp.sum(
            (all_rows[:, None] >= packed_start[None, :]).astype(jnp.int32), axis=1, dtype=jnp.int32
        )
        - 1
    )
    owner_hit = (owner_seq[:, None] == numbers[None, :]).astype(jnp.int32)
    offset = all_rows - jnp.sum(owner_hit * packed_start[None, :], axis=1, dtype=jnp.int32)
    target = jnp.sum(owner_hit * dealing[None, :], axis=1, dtype=jnp.int32)
    target_hit = (target[:, None] == numbers[None, :]).astype(jnp.int32)
    flat_start = bin_start.reshape(total_seqs)
    backward_row = (
        target // per_device * rows_dev
        + jnp.sum(target_hit * flat_start[None, :], axis=1, dtype=jnp.int32)
        + offset
    )
    return (
        source.reshape(total_rows),
        segment.reshape(total_rows),
        position.reshape(total_rows),
        backward_row,
    )


def layer_norm(values, norm_gain, norm_shift):
    center = values - jnp.mean(values, axis=-1, keepdims=True)
    spread = jnp.mean(center * center, axis=-1, keepdims=True)
    return center * lax.rsqrt(spread + EPSILON) * norm_gain + norm_shift


def gelu_tanh(values):
    return jax.nn.gelu(values, approximate=True)


def rows_dot(left, right):
    return lax.dot_general(
        left, right, (((0,), (0,)), ((), ())), preferred_element_type=jnp.float32
    )


def back_dot(left, right):
    return lax.dot_general(
        left, right, (((1,), (1,)), ((), ())), preferred_element_type=jnp.float32
    )


def column_sum(values):
    return jnp.sum(values.astype(jnp.float32), axis=0)


def attention_scores(queries, keys_all, allowed):
    raw_scores = jnp.einsum("qhd,khd->hqk", queries, keys_all, preferred_element_type=jnp.float32)
    return jnp.where(allowed[None], raw_scores * float(HD) ** (-0.5), MASKED)


def take_rows(wanted, carried, pieces):
    row_count = pieces[0].shape[1]
    present = (wanted >= 0) & (wanted < row_count)
    clipped = jnp.clip(wanted, 0, row_count - 1)[:, :, None]
    return tuple(
        (
            jnp.where(
                present[:, :, None], jnp.take_along_axis(shard_rows, clipped, axis=1), previous
            )
            for shard_rows, previous in zip(pieces, carried)
        )
    )


def forward_rows(token_rows, segment, position, weights):
    (
        attention_gain,
        attention_shift,
        input_weight,
        query_bias,
        value_bias,
        output_weight,
        output_bias,
        feed_gain,
        feed_shift,
        up_weight,
        up_bias,
        down_weight,
        down_bias,
    ) = weights
    width = token_rows.shape[1]
    heads = width // HD
    inputs = token_rows.astype(jnp.float32)
    normed, first_back = jax.vjp(
        layer_norm, inputs, attention_gain.astype(jnp.float32), attention_shift.astype(jnp.float32)
    )
    normed_low = normed.astype(jnp.bfloat16)
    mixed = jnp.dot(normed_low, input_weight, preferred_element_type=jnp.float32)
    queries = (
        (mixed[:, :width] + query_bias.astype(jnp.float32))
        .astype(jnp.bfloat16)
        .reshape(-1, heads, HD)
    )
    keys_all = mixed[:, width : 2 * width].astype(jnp.bfloat16).reshape(-1, heads, HD)
    values_all = (
        (mixed[:, 2 * width :] + value_bias.astype(jnp.float32))
        .astype(jnp.bfloat16)
        .reshape(-1, heads, HD)
    )
    allowed = (segment[:, None] == segment[None, :]) & (position[None, :] <= position[:, None])
    scores = attention_scores(queries, keys_all, allowed)
    log_total = jax.nn.logsumexp(scores, axis=-1, keepdims=True)
    soft_low = jnp.exp(scores - log_total).astype(jnp.bfloat16)
    attended = jnp.einsum(
        "hqk,khd->qhd", soft_low, values_all, preferred_element_type=jnp.float32
    ).reshape(-1, width)
    branch = attended.astype(jnp.bfloat16)
    middle = (
        inputs
        + jnp.dot(branch, output_weight, preferred_element_type=jnp.float32)
        + output_bias.astype(jnp.float32)
    )
    normed_two, second_back = jax.vjp(
        layer_norm, middle, feed_gain.astype(jnp.float32), feed_shift.astype(jnp.float32)
    )
    normed_two_low = normed_two.astype(jnp.bfloat16)
    hidden = jnp.dot(
        normed_two_low, up_weight, preferred_element_type=jnp.float32
    ) + up_bias.astype(jnp.float32)
    activated, gelu_back = jax.vjp(gelu_tanh, hidden)
    activated_low = activated.astype(jnp.bfloat16)
    result = (
        middle
        + jnp.dot(activated_low, down_weight, preferred_element_type=jnp.float32)
        + down_bias.astype(jnp.float32)
    )
    saved_state = (
        normed_low,
        queries,
        keys_all,
        values_all,
        allowed,
        log_total,
        branch,
        normed_two_low,
        activated_low,
        first_back,
        second_back,
        gelu_back,
    )
    return (result.astype(jnp.bfloat16), saved_state)


def backward_rows(cotangent_rows, saved_state, matrices):
    input_weight, output_weight, up_weight, down_weight = matrices
    (
        normed_low,
        queries,
        keys_all,
        values_all,
        allowed,
        log_total,
        branch,
        normed_two_low,
        activated_low,
        first_back,
        second_back,
        gelu_back,
    ) = saved_state
    width = branch.shape[1]
    heads = width // HD
    score_scale = float(HD) ** (-0.5)
    upstream = cotangent_rows.astype(jnp.float32)
    down_low = upstream.astype(jnp.bfloat16)
    down_weight_grad = rows_dot(activated_low, down_low)
    down_bias_grad = column_sum(down_low)
    (hidden_grad,) = gelu_back(back_dot(down_low, down_weight))
    hidden_low = hidden_grad.astype(jnp.bfloat16)
    up_weight_grad = rows_dot(normed_two_low, hidden_low)
    up_bias_grad = column_sum(hidden_low)
    feed_part, feed_gain_grad, feed_shift_grad = second_back(back_dot(hidden_low, up_weight))
    middle_grad = upstream + feed_part
    output_low = middle_grad.astype(jnp.bfloat16)
    output_weight_grad = rows_dot(branch, output_low)
    output_bias_grad = column_sum(output_low)
    attended_low = back_dot(output_low, output_weight).astype(jnp.bfloat16).reshape(-1, heads, HD)
    scores = attention_scores(queries, keys_all, allowed)
    soft = jnp.exp(scores - log_total)
    soft_grad = jnp.einsum(
        "qhd,khd->hqk", attended_low, values_all, preferred_element_type=jnp.float32
    )
    score_low = (soft * (soft_grad - jnp.sum(soft * soft_grad, axis=-1, keepdims=True))).astype(
        jnp.bfloat16
    )
    query_grad = (
        (
            jnp.einsum("hqk,khd->qhd", score_low, keys_all, preferred_element_type=jnp.float32)
            * score_scale
        )
        .astype(jnp.bfloat16)
        .reshape(-1, width)
    )
    key_grad = (
        (
            jnp.einsum("hqk,qhd->khd", score_low, queries, preferred_element_type=jnp.float32)
            * score_scale
        )
        .astype(jnp.bfloat16)
        .reshape(-1, width)
    )
    value_grad = (
        jnp.einsum(
            "hqk,qhd->khd",
            soft.astype(jnp.bfloat16),
            attended_low,
            preferred_element_type=jnp.float32,
        )
        .astype(jnp.bfloat16)
        .reshape(-1, width)
    )
    mixed_grad = jnp.concatenate([query_grad, key_grad, value_grad], axis=1)
    input_weight_grad = rows_dot(normed_low, mixed_grad)
    inputs_part, attention_gain_grad, attention_shift_grad = first_back(
        back_dot(mixed_grad, input_weight)
    )
    input_grad = (middle_grad + inputs_part).astype(jnp.bfloat16)
    return (
        input_grad,
        (
            attention_gain_grad,
            attention_shift_grad,
            input_weight_grad,
            column_sum(query_grad),
            column_sum(value_grad),
            output_weight_grad,
            output_bias_grad,
            feed_gain_grad,
            feed_shift_grad,
            up_weight_grad,
            up_bias_grad,
            down_weight_grad,
            down_bias_grad,
        ),
    )


def shards(
    tokens,
    cotangent,
    seq_lengths,
    dealing,
    attention_gain,
    attention_shift,
    input_weight,
    query_bias,
    value_bias,
    output_weight,
    output_bias,
    feed_gain,
    feed_shift,
    up_weight,
    up_bias,
    down_weight,
    down_bias,
):
    micro_count, tok_rows, width = tokens.shape
    own_start = lax.axis_index("shard") * tok_rows
    full_maps = jax.vmap(partial(deal_maps, rows_dev=tok_rows))(seq_lengths[:, 0], dealing[:, 0])
    source, segment, position, backward_row = [
        lax.dynamic_slice_in_dim(member, own_start, tok_rows, 1) for member in full_maps
    ]
    empty_rows = jnp.zeros_like(tokens)
    dealt_tokens, dealt_cotangent = take_rows(
        source,
        (empty_rows, empty_rows),
        (
            lax.all_gather(tokens, "shard", axis=1, tiled=True),
            lax.all_gather(cotangent, "shard", axis=1, tiled=True),
        ),
    )
    weights = (
        attention_gain,
        attention_shift,
        input_weight,
        query_bias,
        value_bias,
        output_weight,
        output_bias,
        feed_gain,
        feed_shift,
        up_weight,
        up_bias,
        down_weight,
        down_bias,
    )
    totals = None
    results = []
    input_grads = []
    for micro_step in range(micro_count):
        forward_weights = (
            lax.all_gather(weights[0], "shard", axis=0, tiled=True),
            lax.all_gather(weights[1], "shard", axis=0, tiled=True),
            lax.all_gather(weights[2], "shard", axis=0, tiled=True),
            lax.all_gather(weights[3], "shard", axis=0, tiled=True),
            lax.all_gather(weights[4], "shard", axis=0, tiled=True),
            lax.all_gather(weights[5], "shard", axis=0, tiled=True),
            lax.all_gather(weights[6], "shard", axis=0, tiled=True),
            lax.all_gather(weights[7], "shard", axis=0, tiled=True),
            lax.all_gather(weights[8], "shard", axis=0, tiled=True),
            lax.all_gather(weights[9], "shard", axis=0, tiled=True),
            lax.all_gather(weights[10], "shard", axis=0, tiled=True),
            lax.all_gather(weights[11], "shard", axis=0, tiled=True),
            lax.all_gather(weights[12], "shard", axis=0, tiled=True),
        )
        result, saved_state = forward_rows(
            dealt_tokens[micro_step], segment[micro_step], position[micro_step], forward_weights
        )
        matrices = (
            lax.all_gather(input_weight, "shard", axis=0, tiled=True),
            lax.all_gather(output_weight, "shard", axis=0, tiled=True),
            lax.all_gather(up_weight, "shard", axis=0, tiled=True),
            lax.all_gather(down_weight, "shard", axis=0, tiled=True),
        )
        input_grad, local_grads = backward_rows(dealt_cotangent[micro_step], saved_state, matrices)
        results.append(result)
        input_grads.append(input_grad)
        if micro_step == 0:
            totals = local_grads
        else:
            totals = tuple((earlier + latest for earlier, latest in zip(totals, local_grads)))
    totals = lax.psum_scatter(totals, "shard", scatter_dimension=0, tiled=True)
    totals = lax.psum(totals, "rep")
    restored_out, restored_grad = take_rows(
        backward_row,
        (empty_rows, empty_rows),
        (
            lax.all_gather(jnp.stack(results), "shard", axis=1, tiled=True),
            lax.all_gather(jnp.stack(input_grads), "shard", axis=1, tiled=True),
        ),
    )
    return (restored_out, restored_grad) + tuple(totals)


def solution(mesh):
    return jax.shard_map(
        shards,
        mesh=mesh,
        in_specs=(
            P(None, ("shard", "rep"), None),
            P(None, ("shard", "rep"), None),
            P(None, "rep", None, None),
            P(None, "rep", None),
            P("shard"),
            P("shard"),
            P("shard", None),
            P("shard"),
            P("shard"),
            P("shard", None),
            P("shard"),
            P("shard"),
            P("shard"),
            P("shard", None),
            P("shard"),
            P("shard", None),
            P("shard"),
        ),
        out_specs=(
            P(None, ("shard", "rep"), None),
            P(None, ("shard", "rep"), None),
            P("shard"),
            P("shard"),
            P("shard", None),
            P("shard"),
            P("shard"),
            P("shard", None),
            P("shard"),
            P("shard"),
            P("shard"),
            P("shard", None),
            P("shard"),
            P("shard", None),
            P("shard"),
        ),
        check_vma=False,
    )
```

profile of v0, /device:TPU:0, one launch (start us, length us, event | category | flops | bytes accessed | tf_op | source)
XLA Modules:
  0.0 1307.6 jit_solution(15719994966998990020)
XLA Ops:
  11.6 13.5 %all-gather = bf16[8,1,128]{2,1,0:T(2,128)(2,1)S(1)} all-gather(bf16[1,1,128]{2,1,0:T(2,128)(2,1)S(1)} %bitcast.346), channel_id=1, replica_groups=mesh['shard'=8,'rep'=4] {'shard'}, dimensions={0}, use_global_device_ids=true | all-gather | bytes 2304 | tf_op jit(solution)/shard_map/all_gather | solution.py:329
  34.1 12.6 all-gather.3
  46.8 9.1 all-gather.2
  55.9 12.1 all-gather.4
  67.9 9.1 all-gather.5
  77.0 10.3 all-gather.6
  88.1 14.0 %all-gather.7 = bf16[8,1,512]{2,1,0:T(2,128)(2,1)S(1)} all-gather(bf16[1,1,512]{2,1,0:T(2,128)(2,1)S(1)} %reshape.473), channel_id=1, replica_groups=mesh['shard'=8,'rep'=4] {'shard'}, dimensions={0}, use_global_device_ids=true | all-gather | bytes 9216 | tf_op jit(solution)/shard_map/all_gather | solution.py:339
  112.8 64.0 %all-gather.18.cloned.1.call-done = bf16[2,2048,1024]{2,1,0:T(8,128)(2,1)} async-done(((bf16[2,256,1024]{2,1,0:T(8,128)(2,1)}), bf16[2,2048,1024]{2,1,0:T(8,128)(2,1)}) %all-gather.18.cloned.1.call-update) | async-done | bytes 8388624 | tf_op jit(solution)/shard_map/all_gather | solution.py:305
  176.8 11.2 gather_fusion
  191.2 50.5 %all-gather.20.cloned.1.call-done = bf16[1024,3072]{1,0:T(8,128)(2,1)} async-done(((bf16[128,3072]{1,0:T(8,128)(2,1)}), bf16[1024,3072]{1,0:T(8,128)(2,1)}) %all-gather.20.cloned.1.call-update) | async-done | bytes 6291472 | tf_op jit(solution)/shard_map/all_gather | solution.py:331
  279.5 74.3 %all-gather.24.cloned.1.call-done = bf16[1024,4096]{1,0:T(8,128)(2,1)} async-done(((bf16[128,4096]{1,0:T(8,128)(2,1)}), bf16[1024,4096]{1,0:T(8,128)(2,1)}) %all-gather.24.cloned.1.call-update) | async-done | bytes 8388624 | tf_op jit(solution)/shard_map/all_gather | solution.py:338
  366.6 69.2 %all-gather.26.cloned.1.call-done = bf16[4096,1024]{1,0:T(8,128)(2,1)} async-done(((bf16[512,1024]{1,0:T(8,128)(2,1)}), bf16[4096,1024]{1,0:T(8,128)(2,1)}) %all-gather.26.cloned.1.call-update) | async-done | bytes 8388624 | tf_op jit(solution)/shard_map/all_gather | solution.py:340
  507.3 11.0 fusion.65
  518.4 11.7 convolution_add_fusion
  534.6 10.1 convolution_add_fusion.1
  545.4 9.3 all-gather.8
  584.1 65.0 %reduce-scatter.5.cloned.1.call-done = f32[128,3072]{1,0:T(8,128)} async-done(((f32[1024,3072]{1,0:T(8,128)}), f32[128,3072]{1,0:T(8,128)}) %reduce-scatter.5.cloned.1.call-update) | async-done | bytes 1572880 | tf_op jit(solution)/shard_map/reduce_scatter | solution.py:359
  649.1 169.0 %reduce-scatter.11.cloned.1.call-done = f32[512,1024]{1,0:T(8,128)} async-done(((f32[4096,1024]{1,0:T(8,128)}), f32[512,1024]{1,0:T(8,128)}) %reduce-scatter.11.cloned.1.call-update) | async-done | bytes 2097168 | tf_op jit(solution)/shard_map/reduce_scatter | solution.py:359
  818.1 168.9 %reduce-scatter.9.cloned.1.call-done = f32[128,4096]{1,0:T(8,128)} async-done(((f32[1024,4096]{1,0:T(8,128)}), f32[128,4096]{1,0:T(8,128)}) %reduce-scatter.9.cloned.1.call-update) | async-done | bytes 2097168 | tf_op jit(solution)/shard_map/reduce_scatter | solution.py:359
  989.3 28.7 %all-reduce.9 = (f32[1024]{0:T(1024)S(1)}, f32[1024]{0:T(1024)S(1)}, f32[1024]{0:T(1024)S(1)}, f32[1024]{0:T(1024)S(1)}, f32[1024]{0:T(1024)S(1)}, /*index=5*/f3...) all-reduce(f32[1024]{0:T(1024)S(1)} %add.367, ...), channel_id=2, replica_groups=mesh['shard'=8,'rep'=4] {'shard'}, use_global_device_ids=true, to_apply=%region_35.37.clone | all-reduce | flops 12288 | bytes 98304
  1018.7 10.8 all-reduce.10
  1029.5 41.0 %all-gather.28.cloned.1.call-done = bf16[2,2048,1024]{2,1,0:T(8,128)(2,1)} async-done(((bf16[2,256,1024]{2,1,0:T(8,128)(2,1)}), bf16[2,2048,1024]{2,1,0:T(8,128)(2,1)}) %all-gather.28.cloned.1.call-update) | async-done | bytes 8388624 | tf_op jit(solution)/shard_map/all_gather | solution.py:365
  1078.6 74.4 %all-gather.32.cloned.1.call-done = bf16[2,2048,1024]{2,1,0:T(8,128)(2,1)} async-done(((bf16[2,256,1024]{2,1,0:T(8,128)(2,1)}), bf16[2,2048,1024]{2,1,0:T(8,128)(2,1)}) %all-gather.32.cloned.1.call-update) | async-done | bytes 8388624 | tf_op jit(solution)/shard_map/all_gather | solution.py:366
  1162.7 130.7 %all-reduce.14.cloned.1.call-done = (f32[128,3072]{1,0:T(8,128)}, f32[128,1024]{1,0:T(8,128)}, f32[128,4096]{1,0:T(8,128)}, f32[512,1024]{1,0:T(8,128)}) async-done(((f32[128,3072]{1,0:T(8,128)}, f32[128,1024]{1,0:T(8,128)}, f32[128,4096]{1,0:T(8,128)}, f32[512,1024]{1,0:T(8,128)}), (f32[128,3072]{1,0:T(8,128)}, f32[128,1024]{1,0:T(8,128)}, f32[128,4096]{1,0:T(8,128)}, ...) | async-done | bytes 6291472 | tf_op jit(solution)/shard_map/psum | solution.py:360
  (372 shorter events, 210.0 us)
Async XLA Ops:
  7.3 97.4 %all-gather.30.cloned.1.call-start = ((), (), s32[]{:S(2)}) async-start(), calls=%async_computation.10 | async-start | bytes 9437184 | tf_op jit(solution)/shard_map/all_gather | solution.py:306
  8.0 168.8 %all-gather.18.cloned.1.call-start = ((), (), s32[]{:S(2)}) async-start(), calls=%async_computation.4 | async-start | bytes 9437184 | tf_op jit(solution)/shard_map/all_gather | solution.py:305
  8.8 232.9 %all-gather.20.cloned.1.call-start = ((), (), s32[]{:S(2)}) async-start(), calls=%async_computation.5 | async-start | bytes 7077888 | tf_op jit(solution)/shard_map/all_gather | solution.py:331
  9.5 261.4 %all-gather.22.cloned.1.call-start = ((), (), s32[]{:S(2)}) async-start(), calls=%async_computation.6 | async-start | bytes 2359296 | tf_op jit(solution)/shard_map/all_gather | solution.py:334
  10.1 343.8 %all-gather.24.cloned.1.call-start = ((), (), s32[]{:S(2)}) async-start(), calls=%async_computation.7 | async-start | bytes 9437184 | tf_op jit(solution)/shard_map/all_gather | solution.py:338
  10.7 425.2 %all-gather.26.cloned.1.call-start = ((), (), s32[]{:S(2)}) async-start(), calls=%async_computation.8 | async-start | bytes 9437184 | tf_op jit(solution)/shard_map/all_gather | solution.py:340
  11.2 572.9 %reduce-scatter.7.cloned.1.call-start = ((), (), s32[]{:S(2)}) async-start(), calls=%async_computation.13 | async-start | bytes 4718592 | tf_op jit(solution)/shard_map/reduce_scatter | solution.py:359
  470.6 178.5 %reduce-scatter.5.cloned.1.call-start = ((), (), s32[]{:S(2)}) async-start(), calls=%async_computation.12 | async-start | bytes 14155776 | tf_op jit(solution)/shard_map/reduce_scatter | solution.py:359
  507.2 310.9 %reduce-scatter.11.cloned.1.call-start = ((), (), s32[]{:S(2)}) async-start(), calls=%async_computation.15 | async-start | bytes 18874368 | tf_op jit(solution)/shard_map/reduce_scatter | solution.py:359
  530.1 456.9 %reduce-scatter.9.cloned.1.call-start = ((), (), s32[]{:S(2)}) async-start(), calls=%async_computation.14 | async-start | bytes 18874368 | tf_op jit(solution)/shard_map/reduce_scatter | solution.py:359
  544.8 525.7 %all-gather.28.cloned.1.call-start = ((), (), s32[]{:S(2)}) async-start(), calls=%async_computation.9 | async-start | bytes 9437184 | tf_op jit(solution)/shard_map/all_gather | solution.py:365
  570.1 582.9 %all-gather.32.cloned.1.call-start = ((), (), s32[]{:S(2)}) async-start(), calls=%async_computation.11 | async-start | bytes 9437184 | tf_op jit(solution)/shard_map/all_gather | solution.py:366
  583.9 405.2 %copy-start.49 = (f32[16,64]{1,0:T(8,128)S(1)}, f32[16,64]{1,0:T(8,128)}, u32[]{:S(2)}) copy-start(f32[16,64]{1,0:T(8,128)} %get-tuple-element.121) | copy-start | bytes 12292
  583.9 405.3 %copy-start.57 = (f32[4096]{0:T(1024)S(1)}, f32[4096]{0:T(1024)}, u32[]{:S(2)}) copy-start(f32[4096]{0:T(1024)} %get-tuple-element.129) | copy-start | bytes 49156
  583.9 405.2 %copy-start.58 = (f32[4096]{0:T(1024)S(1)}, f32[4096]{0:T(1024)}, u32[]{:S(2)}) copy-start(f32[4096]{0:T(1024)} %get-tuple-element.131) | copy-start | bytes 49156
  583.9 405.2 %copy-start.78 = (f32[1024]{0:T(1024)S(1)}, f32[1024]{0:T(1024)}, u32[]{:S(2)}) copy-start(f32[1024]{0:T(1024)} %get-tuple-element.22) | copy-start | bytes 12292
  583.9 405.2 %copy-start.79 = (f32[1024]{0:T(1024)S(1)}, f32[1024]{0:T(1024)}, u32[]{:S(2)}) copy-start(f32[1024]{0:T(1024)} %get-tuple-element.102) | copy-start | bytes 12292
  583.9 405.3 %copy-start.76 = (f32[1024]{0:T(1024)S(1)}, f32[1024]{0:T(1024)}, u32[]{:S(2)}) copy-start(f32[1024]{0:T(1024)} %get-tuple-element.32) | copy-start | bytes 12292
  584.0 405.3 %copy-start.77 = (f32[1024]{0:T(1024)S(1)}, f32[1024]{0:T(1024)}, u32[]{:S(2)}) copy-start(f32[1024]{0:T(1024)} %get-tuple-element.100) | copy-start | bytes 12292
  584.0 405.3 %copy-start.61 = (f32[1024]{0:T(1024)S(1)}, f32[1024]{0:T(1024)}, u32[]{:S(2)}) copy-start(f32[1024]{0:T(1024)} %get-tuple-element.29) | copy-start | bytes 12292
  584.0 405.3 %copy-start.62 = (f32[1024]{0:T(1024)S(1)}, f32[1024]{0:T(1024)}, u32[]{:S(2)}) copy-start(f32[1024]{0:T(1024)} %get-tuple-element.30) | copy-start | bytes 12292
  584.0 405.3 %copy-start.59 = (f32[1024]{0:T(1024)S(1)}, f32[1024]{0:T(1024)}, u32[]{:S(2)}) copy-start(f32[1024]{0:T(1024)} %get-tuple-element.82) | copy-start | bytes 12292
  584.0 405.3 %copy-start.60 = (f32[1024]{0:T(1024)S(1)}, f32[1024]{0:T(1024)}, u32[]{:S(2)}) copy-start(f32[1024]{0:T(1024)} %get-tuple-element.84) | copy-start | bytes 12292
  584.0 709.4 %all-reduce.14.cloned.1.call-start = ((), (), s32[]{:S(2)}) async-start(), calls=%async_computation.16 | async-start | bytes 12582912 | tf_op jit(solution)/shard_map/psum | solution.py:360
  (82 other events, 4319.1 us)
Sparse Core Ops, SparseCore 0:
  9.7 84.8 all-gather.29
  96.2 80.5 all-gather.17
  178.4 63.1 all-gather.19
  243.1 27.7 all-gather.21
  272.4 81.4 all-gather.23
  355.3 80.5 all-gather.25
  470.7 48.3 reduce-scatter.6
  521.4 127.6 reduce-scatter.4
  651.5 166.6 reduce-scatter.10
  820.3 166.6 reduce-scatter.8
  989.2 81.2 all-gather.27
  1072.5 80.4 all-gather.31
  1156.7 136.6 all-reduce.13
where the time goes:
time: 1310 us
  waiting for transfers between devices  913 us (70%)
  matrix products  152 us (12%)
  blocking collectives  138 us (11%)
  local copies, waits for them, and re-layouts  63.7 us (5%)
  other arithmetic  22.4 us (2%)
  between operations  17 us (1%)
    reduce_scatter x4, waiting for transfers between devices, shards(): totals = lax.psum_scatter(totals, 'shard', scatter_dimension=0, tiled=True)  403 us
    psum x1, waiting for transfers between devices, shards(): totals = lax.psum(totals, 'rep')  131 us
    all_gather x1, waiting for transfers between devices, shards(): lax.all_gather(jnp.stack(input_grads), 'shard', axis=1, tiled=True)  74.4 us
    all_gather x1, waiting for transfers between devices, shards(): lax.all_gather(weights[9], 'shard', axis=0, tiled=True)  74.3 us
    all_gather x1, waiting for transfers between devices, shards(): lax.all_gather(weights[11], 'shard', axis=0, tiled=True)  69.2 us
    all_gather x1, waiting for transfers between devices, shards(): lax.all_gather(tokens, 'shard', axis=1, tiled=True)  64 us
    all_gather x1, waiting for transfers between devices, shards(): lax.all_gather(weights[2], 'shard', axis=0, tiled=True)  50.5 us
    dot_general x8, matrix products, rows_dot(): lax.dot_general(left, right, (((0,), (0,)), ((), ())), preferred_element_...  50 us
  transfers between devices with their start and end apart: 13, of which 11 were waited for; matrix products, arithmetic and copies ran while one was open for 14% of the time, Pallas kernels for 0%

commit v1 on v0

--- a/solution.py
+++ b/solution.py
@@ -1,3 +1,4 @@
+import functools
 from functools import partial
 import jax
 import jax.numpy as jnp
@@ -7,6 +8,37 @@
 HD = 64
 EPSILON = 1e-05
 MASKED = -1e30
+
+
+def guide_fields(vector, net_axis, in_dim):
+    seen_now, placed, s_next = (
+        lax.axis_size(net_axis),
+        lax.axis_index(net_axis),
+        vector.shape[in_dim],
+    )
+    store = [p * seen_now if s == in_dim else p for s, p in enumerate(vector.shape)]
+    block_last = z1 = vector
+    src_i = 1
+    next_value = lax.dynamic_update_slice_in_dim(
+        jnp.zeros(store, vector.dtype), vector, placed * s_next, axis=in_dim
+    )
+    while src_i < seen_now // 2 + 1:
+        block_last = lax.ppermute(
+            block_last, net_axis, [(s, (s + 1) % seen_now) for s in range(seen_now)]
+        )
+        next_value = lax.dynamic_update_slice_in_dim(
+            next_value, block_last, (placed - src_i) % seen_now * s_next, axis=in_dim
+        )
+        if 2 * src_i < seen_now:
+            z1 = lax.ppermute(z1, net_axis, [(s, (s - 1) % seen_now) for s in range(seen_now)])
+            next_value = lax.dynamic_update_slice_in_dim(
+                next_value, z1, (placed + src_i) % seen_now * s_next, axis=in_dim
+            )
+        src_i += 1
+    return next_value
+
+
+matrix_check = functools.partial(guide_fields, net_axis="shard", in_dim=1)
 
 
 def deal_maps(seq_lengths, dealing, rows_dev):
@@ -362,7 +394,7 @@
         backward_row,
         (empty_rows, empty_rows),
         (
-            lax.all_gather(jnp.stack(results), "shard", axis=1, tiled=True),
+            matrix_check(jnp.stack(results)),
             lax.all_gather(jnp.stack(input_grads), "shard", axis=1, tiled=True),
         ),
     )

time: 1310 us -> 1280 us (0.977)
  waiting for transfers between devices: 913 us -> 834 us
  local copies, waits for them, and re-layouts: 63.7 us -> 80.6 us
  starting transfers between devices: 0.73 us -> 15.9 us
    ppermute x0 -> x7, waiting for transfers between devices: none -> 104 us  [the longest x4 94.7 us: guide_fields(): lax.ppermute(block_last, net_axis, [(s, (s + 1) % seen_now) for s in rang...]
    psum x1, waiting for transfers between devices: 131 us -> 47.9 us  [shards(): totals = lax.psum(totals, 'rep')]
    all_gather x1, waiting for transfers between devices: 74.4 us -> 0.02 us  [shards(): lax.all_gather(jnp.stack(input_grads), 'shard', axis=1, tiled=True)]
    all_gather x1 -> x0, waiting for transfers between devices: 41 us -> none  [shards(): lax.all_gather(jnp.stack(results), 'shard', axis=1, tiled=True)]
    reduce_scatter x4, waiting for transfers between devices: 403 us -> 418 us  [shards(): totals = lax.psum_scatter(totals, 'shard', scatter_dimension=0, tiled=True)]
    ppermute x0 -> x7, starting transfers between devices: none -> 15.1 us  [the longest x3 10.9 us: guide_fields(): lax.ppermute(z1, net_axis, [(s, (s - 1) % seen_now) for s in range(seen_n...]
  transfers between devices with their start and end apart: 13 -> 19, of which waited for: 11 -> 13; matrix products, arithmetic and copies ran while one was open for 14% -> 16% of each run, Pallas kernels for 0% -> 0%
where the time goes in v1:
time: 1280 us; the launch traced here: 1270 us
  waiting for transfers between devices  834 us (65%)
  matrix products  153 us (12%)
  blocking collectives  150 us (12%)
  local copies, waits for them, and re-layouts  80.6 us (6%)
  other arithmetic  22.4 us (2%)
  between operations  17.4 us (1%)
  starting transfers between devices  15.9 us (1%)
    reduce_scatter x4, waiting for transfers between devices, shards(): totals = lax.psum_scatter(totals, 'shard', scatter_dimension=0, tiled=True)  418 us
    ppermute x4, waiting for transfers between devices, guide_fields(): lax.ppermute(block_last, net_axis, [(s, (s + 1) % seen_now) for s in rang...  94.7 us
    all_gather x1, waiting for transfers between devices, shards(): lax.all_gather(weights[9], 'shard', axis=0, tiled=True)  74.3 us
    all_gather x1, waiting for transfers between devices, shards(): lax.all_gather(weights[11], 'shard', axis=0, tiled=True)  69.4 us
    all_gather x1, waiting for transfers between devices, shards(): lax.all_gather(tokens, 'shard', axis=1, tiled=True)  64 us
    all_gather x1, waiting for transfers between devices, shards(): lax.all_gather(weights[2], 'shard', axis=0, tiled=True)  50.5 us
    dot_general x8, matrix products, rows_dot(): lax.dot_general(left, right, (((0,), (0,)), ((), ())), preferred_element_...  49.9 us
    psum x1, waiting for transfers between devices, shards(): totals = lax.psum(totals, 'rep')  47.9 us
  transfers between devices with their start and end apart: 19, of which 13 were waited for; matrix products, arithmetic and copies ran while one was open for 16% of the time, Pallas kernels for 0%

profile of v1, /device:TPU:0, one launch (start us, length us, event | category | flops | bytes accessed | tf_op | source)
XLA Modules:
  0.0 1273.3 jit_solution(7219356738197048274)
XLA Ops:
  11.6 13.5 %all-gather = bf16[8,1,128]{2,1,0:T(2,128)(2,1)S(1)} all-gather(bf16[1,1,128]{2,1,0:T(2,128)(2,1)S(1)} %bitcast.346), channel_id=1, replica_groups=mesh['shard'=8,'rep'=4] {'shard'}, dimensions={0}, use_global_device_ids=true | all-gather | bytes 2304 | tf_op jit(solution)/shard_map/all_gather | solution.py:361
  34.1 12.6 all-gather.3
  55.9 12.1 all-gather.4
  67.9 9.1 all-gather.5
  77.0 10.3 all-gather.6
  88.1 14.0 %all-gather.7 = bf16[8,1,512]{2,1,0:T(2,128)(2,1)S(1)} all-gather(bf16[1,1,512]{2,1,0:T(2,128)(2,1)S(1)} %reshape.473), channel_id=1, replica_groups=mesh['shard'=8,'rep'=4] {'shard'}, dimensions={0}, use_global_device_ids=true | all-gather | bytes 9216 | tf_op jit(solution)/shard_map/all_gather | solution.py:371
  112.8 64.0 %all-gather.17.cloned.1.call-done = bf16[2,2048,1024]{2,1,0:T(8,128)(2,1)} async-done(((bf16[2,256,1024]{2,1,0:T(8,128)(2,1)}), bf16[2,2048,1024]{2,1,0:T(8,128)(2,1)}) %all-gather.17.cloned.1.call-update) | async-done | bytes 8388624 | tf_op jit(solution)/shard_map/all_gather | solution.py:337
  176.8 11.2 gather_fusion
  191.2 50.5 %all-gather.19.cloned.1.call-done = bf16[1024,3072]{1,0:T(8,128)(2,1)} async-done(((bf16[128,3072]{1,0:T(8,128)(2,1)}), bf16[1024,3072]{1,0:T(8,128)(2,1)}) %all-gather.19.cloned.1.call-update) | async-done | bytes 6291472 | tf_op jit(solution)/shard_map/all_gather | solution.py:363
  279.5 74.3 %all-gather.23.cloned.1.call-done = bf16[1024,4096]{1,0:T(8,128)(2,1)} async-done(((bf16[128,4096]{1,0:T(8,128)(2,1)}), bf16[1024,4096]{1,0:T(8,128)(2,1)}) %all-gather.23.cloned.1.call-update) | async-done | bytes 8388624 | tf_op jit(solution)/shard_map/all_gather | solution.py:370
  366.5 69.4 %all-gather.25.cloned.1.call-done = bf16[4096,1024]{1,0:T(8,128)(2,1)} async-done(((bf16[512,1024]{1,0:T(8,128)(2,1)}), bf16[4096,1024]{1,0:T(8,128)(2,1)}) %all-gather.25.cloned.1.call-update) | async-done | bytes 8388624 | tf_op jit(solution)/shard_map/all_gather | solution.py:372
  507.0 11.0 fusion.65
  518.0 11.8 convolution_add_fusion
  534.3 10.2 convolution_add_fusion.1
  559.5 9.1 all-gather.8
  568.6 80.4 %reduce-scatter.5.cloned.1.call-done = f32[128,3072]{1,0:T(8,128)} async-done(((f32[1024,3072]{1,0:T(8,128)}), f32[128,3072]{1,0:T(8,128)}) %reduce-scatter.5.cloned.1.call-update) | async-done | bytes 1572880 | tf_op jit(solution)/shard_map/reduce_scatter | solution.py:391
  649.0 169.0 %reduce-scatter.11.cloned.1.call-done = f32[512,1024]{1,0:T(8,128)} async-done(((f32[4096,1024]{1,0:T(8,128)}), f32[512,1024]{1,0:T(8,128)}) %reduce-scatter.11.cloned.1.call-update) | async-done | bytes 2097168 | tf_op jit(solution)/shard_map/reduce_scatter | solution.py:391
  818.0 168.9 %reduce-scatter.9.cloned.1.call-done = f32[128,4096]{1,0:T(8,128)} async-done(((f32[1024,4096]{1,0:T(8,128)}), f32[128,4096]{1,0:T(8,128)}) %reduce-scatter.9.cloned.1.call-update) | async-done | bytes 2097168 | tf_op jit(solution)/shard_map/reduce_scatter | solution.py:391
  1010.8 45.8 %collective-permute-done = bf16[2,256,1024]{2,1,0:T(8,128)(2,1)S(1)} collective-permute-done((bf16[2,256,1024]{2,1,0:T(8,128)(2,1)S(1)}, bf16[2,256,1024]{2,1,0:T(8,128)(2,1)S(1)}, u32[]{:S(2)}, u32[]{:S(2)}) %collective-permute-start) | collective-permute-done | bytes 1048608 | tf_op jit(solution)/shard_map/ppermute | solution.py:26
  1060.3 35.9 %collective-permute-done.2 = bf16[2,256,1024]{2,1,0:T(8,128)(2,1)} collective-permute-done((bf16[2,256,1024]{2,1,0:T(8,128)(2,1)S(1)}, bf16[2,256,1024]{2,1,0:T(8,128)(2,1)}, u32[]{:S(2)}, u32[]{:S(2)}) %collective-permute-start.2) | collective-permute-done | bytes 1048608 | tf_op jit(solution)/shard_map/ppermute | solution.py:26
  1111.0 13.0 %collective-permute-done.4 = bf16[2,256,1024]{2,1,0:T(8,128)(2,1)S(1)} collective-permute-done((bf16[2,256,1024]{2,1,0:T(8,128)(2,1)}, bf16[2,256,1024]{2,1,0:T(8,128)(2,1)S(1)}, u32[]{:S(2)}, u32[]{:S(2)}) %collective-permute-start.4) | collective-permute-done | bytes 1048608 | tf_op jit(solution)/shard_map/ppermute | solution.py:26
  1128.4 40.5 %all-reduce.9 = (f32[1024]{0:T(1024)S(1)}, f32[1024]{0:T(1024)S(1)}, f32[1024]{0:T(1024)S(1)}, f32[1024]{0:T(1024)S(1)}, f32[1024]{0:T(1024)S(1)}, /*index=5*/f3...) all-reduce(f32[1024]{0:T(1024)S(1)} %add.441, ...), channel_id=2, replica_groups=mesh['shard'=8,'rep'=4] {'shard'}, use_global_device_ids=true, to_apply=%region_35.37.clone | all-reduce | flops 12288 | bytes 98304
  1169.5 11.3 all-reduce.10
  1211.0 47.9 %all-reduce.14.cloned.1.call-done = (f32[128,3072]{1,0:T(8,128)}, f32[128,1024]{1,0:T(8,128)}, f32[128,4096]{1,0:T(8,128)}, f32[512,1024]{1,0:T(8,128)}) async-done(((f32[128,3072]{1,0:T(8,128)}, f32[128,1024]{1,0:T(8,128)}, f32[128,4096]{1,0:T(8,128)}, f32[512,1024]{1,0:T(8,128)}), (f32[128,3072]{1,0:T(8,128)}, f32[128,1024]{1,0:T(8,128)}, f32[128,4096]{1,0:T(8,128)}, ...) | async-done | bytes 6291472 | tf_op jit(solution)/shard_map/psum | solution.py:392
  (393 shorter events, 260.4 us)
Async XLA Ops:
  7.3 97.4 %all-gather.27.cloned.1.call-start = ((), (), s32[]{:S(2)}) async-start(), calls=%async_computation.9 | async-start | bytes 9437184 | tf_op jit(solution)/shard_map/all_gather | solution.py:338
  8.0 168.8 %all-gather.17.cloned.1.call-start = ((), (), s32[]{:S(2)}) async-start(), calls=%async_computation.4 | async-start | bytes 9437184 | tf_op jit(solution)/shard_map/all_gather | solution.py:337
  8.8 232.9 %all-gather.19.cloned.1.call-start = ((), (), s32[]{:S(2)}) async-start(), calls=%async_computation.5 | async-start | bytes 7077888 | tf_op jit(solution)/shard_map/all_gather | solution.py:363
  9.5 261.4 %all-gather.21.cloned.1.call-start = ((), (), s32[]{:S(2)}) async-start(), calls=%async_computation.6 | async-start | bytes 2359296 | tf_op jit(solution)/shard_map/all_gather | solution.py:366
  10.1 343.8 %all-gather.23.cloned.1.call-start = ((), (), s32[]{:S(2)}) async-start(), calls=%async_computation.7 | async-start | bytes 9437184 | tf_op jit(solution)/shard_map/all_gather | solution.py:370
  10.7 425.2 %all-gather.25.cloned.1.call-start = ((), (), s32[]{:S(2)}) async-start(), calls=%async_computation.8 | async-start | bytes 9437184 | tf_op jit(solution)/shard_map/all_gather | solution.py:372
  11.2 557.3 %reduce-scatter.7.cloned.1.call-start = ((), (), s32[]{:S(2)}) async-start(), calls=%async_computation.12 | async-start | bytes 4718592 | tf_op jit(solution)/shard_map/reduce_scatter | solution.py:391
  191.2 309.1 %copy-start.52 = (f32[256]{0:T(256)}, f32[256]{0:T(256)S(1)}, u32[]{:S(2)}) copy-start(f32[256]{0:T(256)S(1)} %fusion.79) | copy-start | bytes 3076
  273.4 190.9 %copy-start.49 = (f32[256]{0:T(256)}, f32[256]{0:T(256)S(1)}, u32[]{:S(2)}) copy-start(f32[256]{0:T(256)S(1)} %broadcast_multiply_fusion.2) | copy-start | bytes 3076
  279.2 185.1 %copy-start.54 = (f32[256]{0:T(256)}, f32[256]{0:T(256)S(1)}, u32[]{:S(2)}) copy-start(f32[256]{0:T(256)S(1)} %broadcast_multiply_fusion) | copy-start | bytes 3076
  279.5 184.8 %copy-start.55 = (f32[256]{0:T(256)}, f32[256]{0:T(256)S(1)}, u32[]{:S(2)}) copy-start(f32[256]{0:T(256)S(1)} %fusion.78) | copy-start | bytes 3076
  470.4 178.6 %reduce-scatter.5.cloned.1.call-start = ((), (), s32[]{:S(2)}) async-start(), calls=%async_computation.11 | async-start | bytes 14155776 | tf_op jit(solution)/shard_map/reduce_scatter | solution.py:391
  506.9 311.1 %reduce-scatter.11.cloned.1.call-start = ((), (), s32[]{:S(2)}) async-start(), calls=%async_computation.14 | async-start | bytes 18874368 | tf_op jit(solution)/shard_map/reduce_scatter | solution.py:391
  529.8 457.0 %reduce-scatter.9.cloned.1.call-start = ((), (), s32[]{:S(2)}) async-start(), calls=%async_computation.13 | async-start | bytes 18874368 | tf_op jit(solution)/shard_map/reduce_scatter | solution.py:391
  544.5 656.8 %all-gather.29.cloned.1.call-start = ((), (), s32[]{:S(2)}) async-start(), calls=%async_computation.10 | async-start | bytes 9437184 | tf_op jit(solution)/shard_map/all_gather | solution.py:398
  559.4 427.5 %copy-start.6 = (f32[256,1024]{1,0:T(8,128)S(1)}, f32[256,1024]{1,0:T(8,128)}, u32[]{:S(2)}) copy-start(f32[256,1024]{1,0:T(8,128)} %copy-done.4) | copy-start | bytes 3145732
  559.4 699.5 %all-reduce.14.cloned.1.call-start = ((), (), s32[]{:S(2)}) async-start(), calls=%async_computation.15 | async-start | bytes 12582912 | tf_op jit(solution)/shard_map/psum | solution.py:392
  1007.3 49.3 %collective-permute-start = (bf16[2,256,1024]{2,1,0:T(8,128)(2,1)S(1)}, bf16[2,256,1024]{2,1,0:T(8,128)(2,1)S(1)}, u32[]{:S(2)}, u32[]{:S(2)}) collective-permute-start(bf16[2,256,1024]{2,1,0:T(8,128)(2,1)S(1)} %get-tuple-element.86), channel_id=1, source_target_pairs={{0,4},{4,8},{8,12},{12,16},{16,20},{20,24},{24,28},{28,0},{1,5},{5... | collective-permute-start | bytes 3145736 | tf_op jit(solution)/shard_map/ppermute | solution.py:26
  1007.3 49.5 %collective-permute-start.1 = (bf16[2,256,1024]{2,1,0:T(8,128)(2,1)S(1)}, bf16[2,256,1024]{2,1,0:T(8,128)(2,1)S(1)}, u32[]{:S(2)}, u32[]{:S(2)}) collective-permute-start(bf16[2,256,1024]{2,1,0:T(8,128)(2,1)S(1)} %get-tuple-element.86), channel_id=1, source_target_pairs={{0,28},{4,0},{8,4},{12,8},{16,12},{20,16},{24,20},{28,24},{1,29},{... | collective-permute-start | bytes 3145736 | tf_op jit(solution)/shard_map/ppermute | solution.py:33
  1056.6 39.7 %collective-permute-start.2 = (bf16[2,256,1024]{2,1,0:T(8,128)(2,1)S(1)}, bf16[2,256,1024]{2,1,0:T(8,128)(2,1)}, u32[]{:S(2)}, u32[]{:S(2)}) collective-permute-start(bf16[2,256,1024]{2,1,0:T(8,128)(2,1)S(1)} %collective-permute-done), channel_id=1, source_target_pairs={{0,4},{4,8},{8,12},{12,16},{16,20},{20,24},{24,28},{28,0},{1,5},{5... | collective-permute-start | bytes 3145736 | tf_op jit(solution)/shard_map/ppermute | solution.py:26
  1056.8 48.4 %collective-permute-start.3 = (bf16[2,256,1024]{2,1,0:T(8,128)(2,1)S(1)}, bf16[2,256,1024]{2,1,0:T(8,128)(2,1)}, u32[]{:S(2)}, u32[]{:S(2)}) collective-permute-start(bf16[2,256,1024]{2,1,0:T(8,128)(2,1)S(1)} %collective-permute-done.1), channel_id=1, source_target_pairs={{0,28},{4,0},{8,4},{12,8},{16,12},{20,16},{24,20},{28,24},{1,29},{... | collective-permute-start | bytes 3145736 | tf_op jit(solution)/shard_map/ppermute | solution.py:33
  1096.2 27.8 %collective-permute-start.4 = (bf16[2,256,1024]{2,1,0:T(8,128)(2,1)}, bf16[2,256,1024]{2,1,0:T(8,128)(2,1)S(1)}, u32[]{:S(2)}, u32[]{:S(2)}) collective-permute-start(bf16[2,256,1024]{2,1,0:T(8,128)(2,1)} %collective-permute-done.2), channel_id=1, source_target_pairs={{0,4},{4,8},{8,12},{12,16},{16,20},{20,24},{24,28},{28,0},{1,5},{5... | collective-permute-start | bytes 3145736 | tf_op jit(solution)/shard_map/ppermute | solution.py:26
  1105.2 83.2 %collective-permute-start.5 = (bf16[2,256,1024]{2,1,0:T(8,128)(2,1)}, bf16[2,256,1024]{2,1,0:T(8,128)(2,1)}, u32[]{:S(2)}, u32[]{:S(2)}) collective-permute-start(bf16[2,256,1024]{2,1,0:T(8,128)(2,1)} %collective-permute-done.3), channel_id=1, source_target_pairs={{0,28},{4,0},{8,4},{12,8},{16,12},{20,16},{24,20},{28,24},{1,29},{... | collective-permute-start | bytes 3145736 | tf_op jit(solution)/shard_map/ppermute | solution.py:33
  1124.0 66.8 %collective-permute-start.6 = (bf16[2,256,1024]{2,1,0:T(8,128)(2,1)S(1)}, bf16[2,256,1024]{2,1,0:T(8,128)(2,1)}, u32[]{:S(2)}, u32[]{:S(2)}) collective-permute-start(bf16[2,256,1024]{2,1,0:T(8,128)(2,1)S(1)} %collective-permute-done.4), channel_id=1, source_target_pairs={{0,4},{4,8},{8,12},{12,16},{16,20},{20,24},{24,28},{28,0},{1,5},{5... | collective-permute-start | bytes 3145736 | tf_op jit(solution)/shard_map/ppermute | solution.py:26
  (89 other events, 3053.6 us)
Sparse Core Ops, SparseCore 0:
  9.7 84.8 all-gather.26
  96.2 80.5 all-gather.16
  178.4 63.1 all-gather.18
  243.1 27.7 all-gather.20
  272.4 81.4 all-gather.22
  355.3 80.5 all-gather.24
  470.5 48.4 reduce-scatter.6
  521.3 127.6 reduce-scatter.4
  651.3 166.6 reduce-scatter.10
  820.2 166.6 reduce-scatter.8
  989.0 125.3 all-gather.28
  1118.0 140.8 all-reduce.13
